TPU v7x, 32 devices: a whole 2x2x4 slice. The times are simulated.
32 devices in a mesh: atom: 8 (over z, x), aux: 4 (over y, core).
Axes of the slice: x: 2, y: 2, z: 4, core: 2. Of those that a mesh axis runs over, the one named last changes fastest.
Arguments:
- three_index: bfloat16 [128, 32, 128, 128], P('atom', 'aux'), may hold values from -6 to 6
- pair_mask: int32 [128, 8, 8], P('atom'), may hold values 0 or 1
- pair_owner: int32 [128, 1], P('atom'), may hold values from 0 to 7; in each aligned block of 16 rows (0 to 15, 16 to 31, ...) at most 2 rows name the same one
- pair_sub: int32 [128], P('atom'), may hold values from 0 to 3
- pair_nu: int32 [128], P('atom'), may hold values from 0 to 31
- live_count: int32 [8], P('atom'), may hold values from 1 to 16, 96 in all
- coefficients: bfloat16 [4096, 128], P('atom'), may hold values from -0.5 to 0.5
- fit_matrix: bfloat16 [32, 32], P('aux'), as said below
Outputs:
- exchange: float32 [4096, 4096], P('atom', 'aux')
Inputs may be any that keep to these rules, and one draw needn't show every extreme that they name: `pair_owner`: among the 16 slots of one atom index, at most 2 name the same owner, and in every draw some owner is named exactly 2 times by some atom index's slots. The first live_count[a] slots of atom index a are live; some atom index has all 16 slots live. `fit_matrix`: Symmetric.
All inputs are finite; a program needn't handle non-finite values. No bound on the sum of `pair_mask` or of `live_count` on one device may be relied on, other than what follows from the above.
Results may differ from a plain program's by a relative error of at most 0.012.
Values may be sent and summed in bfloat16 or wider, within the bound.
A program may use at most 128 MiB of HBM per device.

v0:
```python
import jax
import jax.numpy as jnp
from jax import lax
from jax.sharding import PartitionSpec as P

CAP = 2


def per_device(
    three_index, pair_mask, pair_owner, pair_sub, pair_nu, live_count, coefficients, fit_matrix
):
    slot_count, aux_here, block_size, _ = three_index.shape
    rows_here, occupied = coefficients.shape
    blocks_here = rows_here // block_size
    atom_count = lax.axis_size("atom")
    aux_total = fit_matrix.shape[1]
    basis_total = rows_here * atom_count
    shell_size = block_size // pair_mask.shape[1]
    whole_orbitals = lax.all_gather(coefficients, "atom", axis=0, tiled=True)
    orbital_blocks = whole_orbitals.reshape(basis_total // block_size, block_size, occupied)[
        pair_nu
    ]
    expanded = jnp.repeat(jnp.repeat(pair_mask, shell_size, 1), shell_size, 2).astype(jnp.bfloat16)
    masked = three_index * expanded[:, None, :, :]
    halfway = jnp.einsum(
        "tpmn,tni->tpim", masked, orbital_blocks, preferred_element_type=jnp.float32
    )
    alive_mask = jnp.arange(slot_count) < live_count[0]
    halfway = jnp.where(alive_mask[:, None, None, None], halfway, 0.0).astype(jnp.bfloat16)
    owners = pair_owner[:, 0]
    owner_hits = (owners[:, None] == jnp.arange(atom_count)[None, :]).astype(jnp.int32)
    rank_within = jnp.sum(jnp.cumsum(owner_hits, 0) * owner_hits, 1) - 1
    placement = owners * CAP + rank_within
    routing = (jnp.arange(atom_count * CAP)[:, None] == placement[None, :]).astype(jnp.bfloat16)
    outgoing = jnp.dot(routing, halfway.reshape(slot_count, -1), preferred_element_type=jnp.float32)
    outgoing = outgoing.astype(jnp.bfloat16).reshape(
        atom_count, CAP, aux_here, occupied, block_size
    )
    sub_codes = jnp.dot(
        routing, (pair_sub + 1).astype(jnp.bfloat16)[:, None], preferred_element_type=jnp.float32
    )
    sub_codes = sub_codes.astype(jnp.bfloat16).reshape(atom_count, CAP)
    arrived, arrived_codes = (
        lax.all_to_all(outgoing, "atom", split_axis=0, concat_axis=0, tiled=True),
        lax.all_to_all(sub_codes, "atom", split_axis=0, concat_axis=0, tiled=True),
    )
    wanted = (jnp.arange(blocks_here) + 1).astype(jnp.float32)
    selector = (arrived_codes.reshape(1, -1).astype(jnp.float32) == wanted[:, None]).astype(
        jnp.bfloat16
    )
    gathered_rows = jnp.einsum(
        "sc,cpib->pisb",
        selector,
        arrived.reshape(atom_count * CAP, aux_here, occupied, block_size),
        preferred_element_type=jnp.float32,
    )
    local_rows = gathered_rows.reshape(aux_here, occupied, rows_here).astype(jnp.bfloat16)
    fitted_sum = jnp.einsum(
        "qp,pir->qir",
        fit_matrix,
        lax.all_gather(local_rows, "aux", axis=0, tiled=True),
        preferred_element_type=jnp.float32,
    )
    fitted = fitted_sum.astype(jnp.bfloat16)
    partial_value = lax.dot_general(
        local_rows,
        lax.all_gather(fitted, "atom", axis=2, tiled=True),
        (((0, 1), (0, 1)), ((), ())),
        preferred_element_type=jnp.float32,
    )
    column_part = lax.psum_scatter(
        partial_value.astype(jnp.bfloat16), "aux", scatter_dimension=1, tiled=True
    ).astype(jnp.float32)
    return column_part * (aux_total * occupied) ** (-0.5)


def solution(mesh):
    in_specs = (
        P("atom", "aux", None, None),
        P("atom", None, None),
        P("atom", None),
        P("atom"),
        P("atom"),
        P("atom"),
        P("atom", None),
        P("aux", None),
    )
    out_specs = P("atom", "aux")
    return jax.shard_map(
        per_device, mesh=mesh, in_specs=in_specs, out_specs=out_specs, check_vma=False
    )
```

profile of v0, /device:TPU:0, one launch (start us, length us, event | category | flops | bytes accessed | tf_op | source)
XLA Modules:
  0.0 409.8 jit_solution(733651022336806653)
XLA Ops:
  6.5 0.7 all-gather.4.cloned.1.call-update
  7.3 0.7 fusion.25
  8.0 0.8 select_reduce_fusion
  8.9 0.7 add_add_fusion
  9.5 0.8 fusion.23
  10.3 0.7 all_to_all.12
  11.0 7.3 %all-to-all-start.1 = ((bf16[8,1,2]{2,1,0:T(2,128)(2,1)}), bf16[8,1,2]{2,1,0:T(2,128)(2,1)S(1)}, u32[]{:S(2)}, u32[]{:S(2)}) async-start(bf16[8,1,2]{2,1,0:T(2,128)(2,1)} %all_to_all.12), calls=%async_computation.1 | async-start | bytes 8192 | tf_op jit(solution)/shard_map/all_to_all | solution.py:45
  18.9 0.8 convert_element_type.76
  21.3 31.2 %all-gather.4.cloned.1.call-done = bf16[4096,128]{1,0:T(8,128)(2,1)} async-done(((bf16[512,128]{1,0:T(8,128)(2,1)}), bf16[4096,128]{1,0:T(8,128)(2,1)}) %all-gather.4.cloned.1.call-update) | async-done | bytes 1048592 | tf_op jit(solution)/shard_map/all_gather | solution.py:19
  52.5 1.9 gather_fusion
  54.4 4.1 select_convert_fusion
  58.4 2.5 fusion.12
  61.0 2.7 copy.31
  63.7 4.5 %all-to-all-start = ((bf16[8,2,8,128,128]{4,3,2,1,0:T(8,128)(2,1)}), bf16[8,2,8,128,128]{4,3,2,1,0:T(8,128)(2,1)}, u32[]{:S(2)}, u32[]{:S(2)}) async-start(bf16[8,2,8,128,128]{4,3,2,1,0:T(8,128)(2,1)} %bitcast.52), calls=%async_computation | async-start | bytes 8388608 | tf_op jit(solution)/shard_map/all_to_all | solution.py:44
  68.6 91.4 %all-to-all-done = bf16[8,2,8,128,128]{4,3,2,1,0:T(8,128)(2,1)} async-done(((bf16[8,2,8,128,128]{4,3,2,1,0:T(8,128)(2,1)}), bf16[8,2,8,128,128]{4,3,2,1,0:T(8,128)(2,1)}, u32[]{:S(2)}, u32[]{:S(2)}) %all-to-all-start) | async-done | bytes 4194336 | tf_op jit(solution)/shard_map/all_to_all | solution.py:44
  160.0 6.5 %copy.20 = bf16[8,2,8,128,128]{4,1,0,3,2:T(2,128)(2,1)S(1)} copy(bf16[8,2,8,128,128]{4,3,2,1,0:T(8,128)(2,1)} %all-to-all-done) | data formatting | bytes 8388608 | tf_op jit(solution)/shard_map/all_to_all | solution.py:44
  166.5 0.8 fusion.19
  167.3 1.2 convert_element_type.89
  168.6 33.6 %all-gather.6.cloned.1.call-done = bf16[32,128,512]{2,1,0:T(8,128)(2,1)} async-done(((bf16[8,128,512]{2,1,0:T(8,128)(2,1)}), bf16[32,128,512]{2,1,0:T(8,128)(2,1)}) %all-gather.6.cloned.1.call-update) | async-done | bytes 4194320 | tf_op jit(solution)/shard_map/all_gather | solution.py:61
  202.2 5.6 %fusion.20 = bf16[8,128,512]{2,0,1:T(8,128)(2,1)} fusion(bf16[32,128,512]{2,1,0:T(8,128)(2,1)} %all-gather.6.cloned.1.call-done, bf16[8,32]{1,0:T(8,128)(2,1)S(1)} %copy-done), kind=kOutput, calls=%fused_computation.18 | convolution fusion | flops 34078720 | bytes 5243392 | tf_op jit(solution)/shard_map/qp,pir->qir/dot_general | solution.py:58
  208.1 124.8 %all-gather.8.cloned.1.call-done = bf16[8,128,4096]{2,0,1:T(8,128)(2,1)} async-done(((bf16[8,128,512]{2,0,1:T(8,128)(2,1)}), bf16[8,128,4096]{2,0,1:T(8,128)(2,1)}) %all-gather.8.cloned.1.call-update) | async-done | bytes 8388624 | tf_op jit(solution)/shard_map/all_gather | solution.py:67
  332.9 24.8 %bitcast_convert_fusion = bf16[512,4096]{1,0:T(8,128)(2,1)} fusion(bf16[8,128,512]{2,1,0:T(8,128)(2,1)S(1)} %copy-done.1, bf16[8,128,4096]{2,0,1:T(8,128)(2,1)} %all-gather.8.cloned.1.call-done), kind=kOutput, calls=%fused_computation.2 | convolution fusion | flops 4297064448 | bytes 13631488 | tf_op jit(solution)/shard_map/dot_general | solution.py:65
  357.7 42.8 %reduce-scatter.2.cloned.1.call-done = bf16[512,1024]{1,0:T(8,128)(2,1)} async-done(((bf16[512,4096]{1,0:T(8,128)(2,1)}), bf16[512,1024]{1,0:T(8,128)(2,1)}) %reduce-scatter.2.cloned.1.call-update) | async-done | bytes 1048592 | tf_op jit(solution)/shard_map/reduce_scatter | solution.py:71
  400.5 2.8 convert_multiply_fusion
  (24 shorter events, 2.3 us)
Async XLA Ops:
  6.5 195.6 %copy-start = (bf16[8,32]{1,0:T(8,128)(2,1)S(1)}, bf16[8,32]{1,0:T(8,128)(2,1)}, u32[]{:S(2)}) copy-start(bf16[8,32]{1,0:T(8,128)(2,1)} %param.15) | copy-start | bytes 1540
  6.5 46.0 %all-gather.4.cloned.1.call-start = ((), (), s32[]{:S(2)}) async-start(), calls=%async_computation.3 | async-start | bytes 1179648 | tf_op jit(solution)/shard_map/all_gather | solution.py:19
  11.0 52.7 %all-to-all-start.1 = ((bf16[8,1,2]{2,1,0:T(2,128)(2,1)}), bf16[8,1,2]{2,1,0:T(2,128)(2,1)S(1)}, u32[]{:S(2)}, u32[]{:S(2)}) async-start(bf16[8,1,2]{2,1,0:T(2,128)(2,1)} %all_to_all.12), calls=%async_computation.1 | async-start | bytes 8192 | tf_op jit(solution)/shard_map/all_to_all | solution.py:45
  63.7 96.3 %all-to-all-start = ((bf16[8,2,8,128,128]{4,3,2,1,0:T(8,128)(2,1)}), bf16[8,2,8,128,128]{4,3,2,1,0:T(8,128)(2,1)}, u32[]{:S(2)}, u32[]{:S(2)}) async-start(bf16[8,2,8,128,128]{4,3,2,1,0:T(8,128)(2,1)} %bitcast.52), calls=%async_computation | async-start | bytes 8388608 | tf_op jit(solution)/shard_map/all_to_all | solution.py:44
  68.3 133.9 %all-gather.6.cloned.1.call-start = ((), (), s32[]{:S(2)}) async-start(), calls=%async_computation.4 | async-start | bytes 5242880 | tf_op jit(solution)/shard_map/all_gather | solution.py:61
  168.5 164.4 %copy-start.1 = (bf16[8,128,512]{2,1,0:T(8,128)(2,1)S(1)}, bf16[8,128,512]{2,1,0:T(8,128)(2,1)}, u32[]{:S(2)}) copy-start(bf16[8,128,512]{2,1,0:T(8,128)(2,1)} %convert_element_type.89) | copy-start | bytes 3145732
  168.5 164.4 %all-gather.8.cloned.1.call-start = ((), (), s32[]{:S(2)}) async-start(), calls=%async_computation.5 | async-start | bytes 9437184 | tf_op jit(solution)/shard_map/all_gather | solution.py:67
  207.8 192.7 %reduce-scatter.2.cloned.1.call-start = ((), (), s32[]{:S(2)}) async-start(), calls=%async_computation.6 | async-start | bytes 5242880 | tf_op jit(solution)/shard_map/reduce_scatter | solution.py:71
Sparse Core Ops, SparseCore 0:
  9.5 42.9 all-gather.3
  168.7 33.4 all-gather.5
  207.9 124.9 all-gather.7
  357.8 42.5 reduce-scatter.1
where the time goes:
time: 410 us
  waiting for transfers between devices  325 us (79%)
  matrix products  38.5 us (9%)
  local copies, waits for them, and re-layouts  14 us (3%)
  between operations  13.9 us (3%)
  starting transfers between devices  12.4 us (3%)
  other arithmetic  6.54 us (2%)
    all_gather x1, waiting for transfers between devices, per_device(): lax.all_gather(fitted, 'atom', axis=2, tiled=True)  125 us
    all_to_all x1, waiting for transfers between devices, per_device(): lax.all_to_all(outgoing, 'atom', split_axis=0, concat_axis=0, tiled=True)  91.4 us
    reduce_scatter x1, waiting for transfers between devices, per_device(): lax.psum_scatter(partial_value.astype(jnp.bfloat16), 'aux', scatter_dimen...  42.8 us
    all_gather x1, waiting for transfers between devices, per_device(): lax.all_gather(local_rows, 'aux', axis=0, tiled=True)  33.6 us
    all_gather x1, waiting for transfers between devices, per_device(): whole_orbitals = lax.all_gather(coefficients, 'atom', axis=0, tiled=True)  31.2 us
    dot_general x1, matrix products, per_device(): lax.dot_general(local_rows, lax.all_gather(fitted, 'atom', axis=2, tiled=...  24.8 us
  transfers between devices with their start and end apart: 6, of which 5 were waited for; matrix products, arithmetic and copies ran while one was open for 4% of the time, Pallas kernels for 0%

commit v1 on v0

--- a/solution.py
+++ b/solution.py
@@ -16,7 +16,12 @@
     aux_total = fit_matrix.shape[1]
     basis_total = rows_here * atom_count
     shell_size = block_size // pair_mask.shape[1]
-    whole_orbitals = lax.all_gather(coefficients, "atom", axis=0, tiled=True)
+    ring = [coefficients]
+    for hop in range(7):
+        ring.append(lax.ppermute(ring[-1], "atom", [(dev, (dev + 1) % 8) for dev in range(8)]))
+    whole_orbitals = jnp.roll(
+        jnp.concatenate(ring[::-1], axis=0), (lax.axis_index("atom") + 1) * ring[0].shape[0], axis=0
+    )
     orbital_blocks = whole_orbitals.reshape(basis_total // block_size, block_size, occupied)[
         pair_nu
     ]

time: 410 us -> 416 us (1.015)
    ppermute x0 -> x7, waiting for transfers between devices: none -> 39 us  [per_device(): lax.ppermute(ring[-1], 'atom', [(dev, (dev + 1) % 8) for dev in range(8)])]
    all_gather x1 -> x0, waiting for transfers between devices: 31.2 us -> none  [per_device(): whole_orbitals = lax.all_gather(coefficients, 'atom', axis=0, tiled=True)]
    ppermute x0 -> x7, starting transfers between devices: none -> 5.05 us  [per_device(): lax.ppermute(ring[-1], 'atom', [(dev, (dev + 1) % 8) for dev in range(8)])]
    all_to_all x1, waiting for transfers between devices: 91.4 us -> 86.4 us  [per_device(): lax.all_to_all(outgoing, 'atom', split_axis=0, concat_axis=0, tiled=True)]
  transfers between devices with their start and end apart: 6 -> 12, of which waited for: 5 -> 10; matrix products, arithmetic and copies ran while one was open for 4% -> 4% of each run, Pallas kernels for 0% -> 0%
where the time goes in v1:
time: 416 us; the launch traced here: 415 us
  waiting for transfers between devices  326 us (78%)
  matrix products  38.5 us (9%)
  starting transfers between devices  16.3 us (4%)
  between operations  14 us (3%)
  local copies, waits for them, and re-layouts  13.1 us (3%)
  other arithmetic  6.53 us (2%)
    all_gather x1, waiting for transfers between devices, per_device(): lax.all_gather(fitted, 'atom', axis=2, tiled=True)  125 us
    all_to_all x1, waiting for transfers between devices, per_device(): lax.all_to_all(outgoing, 'atom', split_axis=0, concat_axis=0, tiled=True)  86.4 us
    reduce_scatter x1, waiting for transfers between devices, per_device(): lax.psum_scatter(partial_value.astype(jnp.bfloat16), 'aux', scatter_dimen...  42.8 us
    ppermute x7, waiting for transfers between devices, per_device(): lax.ppermute(ring[-1], 'atom', [(dev, (dev + 1) % 8) for dev in range(8)])  39 us
    all_gather x1, waiting for transfers between devices, per_device(): lax.all_gather(local_rows, 'aux', axis=0, tiled=True)  33.4 us
    dot_general x1, matrix products, per_device(): lax.dot_general(local_rows, lax.all_gather(fitted, 'atom', axis=2, tiled=...  24.8 us
  transfers between devices with their start and end apart: 12, of which 10 were waited for; matrix products, arithmetic and copies ran while one was open for 4% of the time, Pallas kernels for 0%

profile of v1, /device:TPU:0, one launch (start us, length us, event | category | flops | bytes accessed | tf_op | source)
XLA Modules:
  0.0 415.0 jit_solution(16496509812206694696)
XLA Ops:
  6.5 3.0 collective-permute-start
  9.5 6.7 %collective-permute-done = bf16[512,128]{1,0:T(8,128)(2,1)S(1)} collective-permute-done((bf16[512,128]{1,0:T(8,128)(2,1)}, bf16[512,128]{1,0:T(8,128)(2,1)S(1)}, u32[]{:S(2)}, u32[]{:S(2)}) %collective-permute-start) | collective-permute-done | bytes 131104 | tf_op jit(solution)/shard_map/ppermute | solution.py:21
  16.2 7.7 %collective-permute-done.1 = bf16[512,128]{1,0:T(8,128)(2,1)S(1)} collective-permute-done((bf16[512,128]{1,0:T(8,128)(2,1)S(1)}, bf16[512,128]{1,0:T(8,128)(2,1)S(1)}, u32[]{:S(2)}, u32[]{:S(2)}) %collective-permute-start.1) | collective-permute-done | bytes 131104 | tf_op jit(solution)/shard_map/ppermute | solution.py:21
  24.7 0.8 select_reduce_fusion
  25.5 6.1 %collective-permute-done.2 = bf16[512,128]{1,0:T(8,128)(2,1)S(1)} collective-permute-done((bf16[512,128]{1,0:T(8,128)(2,1)S(1)}, bf16[512,128]{1,0:T(8,128)(2,1)S(1)}, u32[]{:S(2)}, u32[]{:S(2)}) %collective-permute-start.2) | collective-permute-done | bytes 131104 | tf_op jit(solution)/shard_map/ppermute | solution.py:21
  32.2 7.0 %collective-permute-done.3 = bf16[512,128]{1,0:T(8,128)(2,1)S(1)} collective-permute-done((bf16[512,128]{1,0:T(8,128)(2,1)S(1)}, bf16[512,128]{1,0:T(8,128)(2,1)S(1)}, u32[]{:S(2)}, u32[]{:S(2)}) %collective-permute-start.3) | collective-permute-done | bytes 131104 | tf_op jit(solution)/shard_map/ppermute | solution.py:21
  39.2 0.8 fusion.23
  40.7 6.1 %all-to-all-start.1 = ((bf16[8,1,2]{2,1,0:T(2,128)(2,1)}), bf16[8,1,2]{2,1,0:T(2,128)(2,1)S(1)}, u32[]{:S(2)}, u32[]{:S(2)}) async-start(bf16[8,1,2]{2,1,0:T(2,128)(2,1)} %all_to_all.12), calls=%async_computation.1 | async-start | bytes 8192 | tf_op jit(solution)/shard_map/all_to_all | solution.py:50
  47.5 2.1 collective-permute-start.5
  50.2 5.6 %collective-permute-done.5 = bf16[512,128]{1,0:T(8,128)(2,1)S(1)} collective-permute-done((bf16[512,128]{1,0:T(8,128)(2,1)S(1)}, bf16[512,128]{1,0:T(8,128)(2,1)S(1)}, u32[]{:S(2)}, u32[]{:S(2)}) %collective-permute-start.5) | collective-permute-done | bytes 131104 | tf_op jit(solution)/shard_map/ppermute | solution.py:21
  57.5 6.0 %collective-permute-done.6 = bf16[512,128]{1,0:T(8,128)(2,1)S(1)} collective-permute-done((bf16[512,128]{1,0:T(8,128)(2,1)S(1)}, bf16[512,128]{1,0:T(8,128)(2,1)S(1)}, u32[]{:S(2)}, u32[]{:S(2)}) %collective-permute-start.6) | collective-permute-done | bytes 131104 | tf_op jit(solution)/shard_map/ppermute | solution.py:21
  64.7 4.1 select_convert_fusion
  68.7 2.5 fusion.12
  71.3 2.7 copy.31
  74.0 4.5 %all-to-all-start = ((bf16[8,2,8,128,128]{4,3,2,1,0:T(8,128)(2,1)}), bf16[8,2,8,128,128]{4,3,2,1,0:T(8,128)(2,1)}, u32[]{:S(2)}, u32[]{:S(2)}) async-start(bf16[8,2,8,128,128]{4,3,2,1,0:T(8,128)(2,1)} %bitcast.52), calls=%async_computation | async-start | bytes 8388608 | tf_op jit(solution)/shard_map/all_to_all | solution.py:49
  78.9 86.4 %all-to-all-done = bf16[8,2,8,128,128]{4,3,2,1,0:T(8,128)(2,1)} async-done(((bf16[8,2,8,128,128]{4,3,2,1,0:T(8,128)(2,1)}), bf16[8,2,8,128,128]{4,3,2,1,0:T(8,128)(2,1)}, u32[]{:S(2)}, u32[]{:S(2)}) %all-to-all-start) | async-done | bytes 4194336 | tf_op jit(solution)/shard_map/all_to_all | solution.py:49
  165.3 6.5 %copy.20 = bf16[8,2,8,128,128]{4,1,0,3,2:T(2,128)(2,1)S(1)} copy(bf16[8,2,8,128,128]{4,3,2,1,0:T(8,128)(2,1)} %all-to-all-done) | data formatting | bytes 8388608 | tf_op jit(solution)/shard_map/all_to_all | solution.py:49
  172.6 1.2 convert_element_type.89
  173.9 33.4 %all-gather.3.cloned.1.call-done = bf16[32,128,512]{2,1,0:T(8,128)(2,1)} async-done(((bf16[8,128,512]{2,1,0:T(8,128)(2,1)}), bf16[32,128,512]{2,1,0:T(8,128)(2,1)}) %all-gather.3.cloned.1.call-update) | async-done | bytes 4194320 | tf_op jit(solution)/shard_map/all_gather | solution.py:66
  207.3 5.6 %fusion.20 = bf16[8,128,512]{2,0,1:T(8,128)(2,1)} fusion(bf16[32,128,512]{2,1,0:T(8,128)(2,1)} %all-gather.3.cloned.1.call-done, bf16[8,32]{1,0:T(8,128)(2,1)S(1)} %copy-done), kind=kOutput, calls=%fused_computation.18 | convolution fusion | flops 34078720 | bytes 5243392 | tf_op jit(solution)/shard_map/qp,pir->qir/dot_general | solution.py:63
  213.2 124.8 %all-gather.5.cloned.1.call-done = bf16[8,128,4096]{2,0,1:T(8,128)(2,1)} async-done(((bf16[8,128,512]{2,0,1:T(8,128)(2,1)}), bf16[8,128,4096]{2,0,1:T(8,128)(2,1)}) %all-gather.5.cloned.1.call-update) | async-done | bytes 8388624 | tf_op jit(solution)/shard_map/all_gather | solution.py:72
  338.1 24.8 %bitcast_convert_fusion = bf16[512,4096]{1,0:T(8,128)(2,1)} fusion(bf16[8,128,512]{2,1,0:T(8,128)(2,1)S(1)} %copy-done.1, bf16[8,128,4096]{2,0,1:T(8,128)(2,1)} %all-gather.5.cloned.1.call-done), kind=kOutput, calls=%fused_computation.2 | convolution fusion | flops 4297064448 | bytes 13631488 | tf_op jit(solution)/shard_map/dot_general | solution.py:70
  362.9 42.8 %reduce-scatter.2.cloned.1.call-done = bf16[512,1024]{1,0:T(8,128)(2,1)} async-done(((bf16[512,4096]{1,0:T(8,128)(2,1)}), bf16[512,1024]{1,0:T(8,128)(2,1)}) %reduce-scatter.2.cloned.1.call-update) | async-done | bytes 1048592 | tf_op jit(solution)/shard_map/reduce_scatter | solution.py:76
  405.6 2.8 convert_multiply_fusion
  (54 shorter events, 6.9 us)
Async XLA Ops:
  6.5 200.8 %copy-start = (bf16[8,32]{1,0:T(8,128)(2,1)S(1)}, bf16[8,32]{1,0:T(8,128)(2,1)}, u32[]{:S(2)}) copy-start(bf16[8,32]{1,0:T(8,128)(2,1)} %param.15) | copy-start | bytes 1540
  6.5 9.7 %collective-permute-start = (bf16[512,128]{1,0:T(8,128)(2,1)}, bf16[512,128]{1,0:T(8,128)(2,1)S(1)}, u32[]{:S(2)}, u32[]{:S(2)}) collective-permute-start(bf16[512,128]{1,0:T(8,128)(2,1)} %param.14), channel_id=1, source_target_pairs={{0,4},{4,8},{8,12},{12,16},{16,20},{20,24},{24,28},{28,0},{1,5},{5... | collective-permute-start | bytes 393224 | tf_op jit(solution)/shard_map/ppermute | solution.py:21
  16.2 7.7 %collective-permute-start.1 = (bf16[512,128]{1,0:T(8,128)(2,1)S(1)}, bf16[512,128]{1,0:T(8,128)(2,1)S(1)}, u32[]{:S(2)}, u32[]{:S(2)}) collective-permute-start(bf16[512,128]{1,0:T(8,128)(2,1)S(1)} %collective-permute-done), channel_id=1, source_target_pairs={{0,4},{4,8},{8,12},{12,16},{16,20},{20,24},{24,28},{28,0},{1,5},{5... | collective-permute-start | bytes 393224 | tf_op jit(solution)/shard_map/ppermute | solution.py:21
  23.9 7.7 %collective-permute-start.2 = (bf16[512,128]{1,0:T(8,128)(2,1)S(1)}, bf16[512,128]{1,0:T(8,128)(2,1)S(1)}, u32[]{:S(2)}, u32[]{:S(2)}) collective-permute-start(bf16[512,128]{1,0:T(8,128)(2,1)S(1)} %collective-permute-done.1), channel_id=1, source_target_pairs={{0,4},{4,8},{8,12},{12,16},{16,20},{20,24},{24,28},{28,0},{1,5},{5... | collective-permute-start | bytes 393224 | tf_op jit(solution)/shard_map/ppermute | solution.py:21
  31.6 7.7 %collective-permute-start.3 = (bf16[512,128]{1,0:T(8,128)(2,1)S(1)}, bf16[512,128]{1,0:T(8,128)(2,1)S(1)}, u32[]{:S(2)}, u32[]{:S(2)}) collective-permute-start(bf16[512,128]{1,0:T(8,128)(2,1)S(1)} %collective-permute-done.2), channel_id=1, source_target_pairs={{0,4},{4,8},{8,12},{12,16},{16,20},{20,24},{24,28},{28,0},{1,5},{5... | collective-permute-start | bytes 393224 | tf_op jit(solution)/shard_map/ppermute | solution.py:21
  39.2 8.3 %collective-permute-start.4 = (bf16[512,128]{1,0:T(8,128)(2,1)S(1)}, bf16[512,128]{1,0:T(8,128)(2,1)S(1)}, u32[]{:S(2)}, u32[]{:S(2)}) collective-permute-start(bf16[512,128]{1,0:T(8,128)(2,1)S(1)} %collective-permute-done.3), channel_id=1, source_target_pairs={{0,4},{4,8},{8,12},{12,16},{16,20},{20,24},{24,28},{28,0},{1,5},{5... | collective-permute-start | bytes 393224 | tf_op jit(solution)/shard_map/ppermute | solution.py:21
  40.7 23.0 %copy-start.2 = (bf16[512,128]{1,0:T(8,128)(2,1)S(1)}, bf16[512,128]{1,0:T(8,128)(2,1)}, u32[]{:S(2)}) copy-start(bf16[512,128]{1,0:T(8,128)(2,1)} %param.14) | copy-start | bytes 393220
  40.7 33.3 %all-to-all-start.1 = ((bf16[8,1,2]{2,1,0:T(2,128)(2,1)}), bf16[8,1,2]{2,1,0:T(2,128)(2,1)S(1)}, u32[]{:S(2)}, u32[]{:S(2)}) async-start(bf16[8,1,2]{2,1,0:T(2,128)(2,1)} %all_to_all.12), calls=%async_computation.1 | async-start | bytes 8192 | tf_op jit(solution)/shard_map/all_to_all | solution.py:50
  47.5 8.3 %collective-permute-start.5 = (bf16[512,128]{1,0:T(8,128)(2,1)S(1)}, bf16[512,128]{1,0:T(8,128)(2,1)S(1)}, u32[]{:S(2)}, u32[]{:S(2)}) collective-permute-start(bf16[512,128]{1,0:T(8,128)(2,1)S(1)} %collective-permute-done.4), channel_id=1, source_target_pairs={{0,4},{4,8},{8,12},{12,16},{16,20},{20,24},{24,28},{28,0},{1,5},{5... | collective-permute-start | bytes 393224 | tf_op jit(solution)/shard_map/ppermute | solution.py:21
  55.8 7.7 %collective-permute-start.6 = (bf16[512,128]{1,0:T(8,128)(2,1)S(1)}, bf16[512,128]{1,0:T(8,128)(2,1)S(1)}, u32[]{:S(2)}, u32[]{:S(2)}) collective-permute-start(bf16[512,128]{1,0:T(8,128)(2,1)S(1)} %collective-permute-done.5), channel_id=1, source_target_pairs={{0,4},{4,8},{8,12},{12,16},{16,20},{20,24},{24,28},{28,0},{1,5},{5... | collective-permute-start | bytes 393224 | tf_op jit(solution)/shard_map/ppermute | solution.py:21
  74.0 91.3 %all-to-all-start = ((bf16[8,2,8,128,128]{4,3,2,1,0:T(8,128)(2,1)}), bf16[8,2,8,128,128]{4,3,2,1,0:T(8,128)(2,1)}, u32[]{:S(2)}, u32[]{:S(2)}) async-start(bf16[8,2,8,128,128]{4,3,2,1,0:T(8,128)(2,1)} %bitcast.52), calls=%async_computation | async-start | bytes 8388608 | tf_op jit(solution)/shard_map/all_to_all | solution.py:49
  78.6 128.8 %all-gather.3.cloned.1.call-start = ((), (), s32[]{:S(2)}) async-start(), calls=%async_computation.3 | async-start | bytes 5242880 | tf_op jit(solution)/shard_map/all_gather | solution.py:66
  173.8 164.2 %copy-start.1 = (bf16[8,128,512]{2,1,0:T(8,128)(2,1)S(1)}, bf16[8,128,512]{2,1,0:T(8,128)(2,1)}, u32[]{:S(2)}) copy-start(bf16[8,128,512]{2,1,0:T(8,128)(2,1)} %convert_element_type.89) | copy-start | bytes 3145732
  173.9 164.2 %all-gather.5.cloned.1.call-start = ((), (), s32[]{:S(2)}) async-start(), calls=%async_computation.4 | async-start | bytes 9437184 | tf_op jit(solution)/shard_map/all_gather | solution.py:72
  213.0 192.7 %reduce-scatter.2.cloned.1.call-start = ((), (), s32[]{:S(2)}) async-start(), calls=%async_computation.5 | async-start | bytes 5242880 | tf_op jit(solution)/shard_map/reduce_scatter | solution.py:76
Sparse Core Ops, SparseCore 0:
  174.0 33.3 all-gather.2
  213.1 124.9 all-gather.4
  363.0 42.5 reduce-scatter.1
